TPU v7x, 32 devices: a whole 2x2x4 slice. The times are simulated.
32 devices in a mesh: row: 8 (over z, y), col: 4 (over x, core).
Axes of the slice: x: 2, y: 2, z: 4, core: 2. Of those that a mesh axis runs over, the one named last changes fastest.
Arguments:
- env: float32 [512, 32768], P('row', 'col'), may hold values from -0.03125 to 0.03125
- wave: float32 [32768, 512], P('row', 'col'), may hold values from -6 to 6
- mpo: float32 [16, 16], replicated, may hold values from -1.5 to 1.5
Outputs:
- applied: float32 [512, 512], P('row', 'col')
All inputs are finite; a program needn't handle non-finite values.
Results may differ from a plain program's by a relative error of at most 0.00007.
Values sent between devices are 32-bit elements; how exact they have to be, the bound alone decides.
No kernel may reach another device: no remote copies, remote signals or barrier semaphores. Data moves between devices by JAX's collectives and lax.ppermute only.
A program may use at most 128 MiB of HBM per device.

v0:
```python
import jax
import jax.numpy as jnp
from jax import lax
from jax.sharding import PartitionSpec as P


def shards(env, wave, mpo):
    spins = mpo.shape[0]
    env_full = lax.all_gather(env, "col", axis=1, tiled=True)
    right_local = wave.shape[1] // spins
    partial_out = jnp.dot(
        env_full,
        lax.all_gather(wave, "row", axis=0, tiled=True),
        precision=lax.Precision.HIGHEST,
        preferred_element_type=jnp.float32,
    )
    out3 = partial_out.reshape(env.shape[0], right_local, spins)
    mixed = jnp.einsum("irs,st->itr", out3, mpo, precision=lax.Precision.HIGHEST)
    spun = lax.all_to_all(mixed, "col", split_axis=1, concat_axis=2, tiled=True)
    return spun.reshape(env.shape[0], -1)


def solution(mesh):
    in_specs = (P("row", "col"), P("row", "col"), P())
    out_specs = P("row", "col")
    return jax.shard_map(shards, mesh=mesh, in_specs=in_specs, out_specs=out_specs, check_vma=False)
```

profile of v0, /device:TPU:0, one launch (start us, length us, event | category | flops | bytes accessed | tf_op | source)
XLA Modules:
  0.0 345.3 jit_solution(17700859789182060455)
XLA Ops:
  6.5 0.0 copy-start
  6.5 0.0 all-gather.3.cloned.1.call-start
  6.5 0.7 all-gather.3.cloned.1.call-update
  7.3 0.0 all-gather.5.cloned.1.call-start
  7.3 0.7 all-gather.5.cloned.1.call-update
  8.0 61.9 %all-gather.3.cloned.1.call-done = f32[64,32768]{1,0:T(8,128)} async-done(((f32[64,8192]{1,0:T(8,128)}), f32[64,32768]{1,0:T(8,128)}) %all-gather.3.cloned.1.call-update) | async-done | bytes 8388624 | tf_op jit(solution)/shard_map/all_gather | solution.py:9
  69.9 229.4 %all-gather.5.cloned.1.call-done = f32[32768,128]{1,0:T(8,128)} async-done(((f32[4096,128]{1,0:T(8,128)}), f32[32768,128]{1,0:T(8,128)}) %all-gather.5.cloned.1.call-update) | async-done | bytes 16777232 | tf_op jit(solution)/shard_map/all_gather | solution.py:13
  299.4 30.2 %fusion.1 = f32[64,128]{0,1:T(8,128)S(1)} fusion(f32[64,32768]{1,0:T(8,128)} %all-gather.3.cloned.1.call-done, f32[32768,128]{1,0:T(8,128)} %all-gather.5.cloned.1.call-done), kind=kOutput, calls=%fused_computation.3 | convolution fusion | flops 3221225472 | bytes 25198592 | tf_op jit(solution)/shard_map/dot_general | solution.py:11
  329.5 0.0 copy-done
  329.5 0.3 convolution_bitcast_fusion
  329.8 0.1 reshape.10
  329.9 6.5 %all_to_all.15 = f32[4,1,2048]{2,1,0:T(1,128)S(1)} all-to-all(f32[4,1,2048]{2,1,0:T(1,128)S(1)} %reshape.10), channel_id=1, replica_groups=mesh['row'=8,'col'=4] {'col'}, dimensions={0} | all-to-all | bytes 65536 | tf_op jit(solution)/shard_map/all_to_all | solution.py:19
  336.4 0.5 broadcast
  336.9 0.7 reduce
  337.7 0.1 reshape.11
  337.8 0.7 copy.15
  (2 shorter events, 0.0 us)
Async XLA Ops:
  6.5 323.0 %copy-start = (f32[16,16]{1,0:T(8,128)S(1)}, f32[16,16]{1,0:T(8,128)}, u32[]{:S(2)}) copy-start(f32[16,16]{1,0:T(8,128)} %param.5) | copy-start | bytes 3076
  6.5 63.4 %all-gather.3.cloned.1.call-start = ((), (), s32[]{:S(2)}) async-start(), calls=%async_computation.1 | async-start | bytes 10485760 | tf_op jit(solution)/shard_map/all_gather | solution.py:9
  7.3 292.1 %all-gather.5.cloned.1.call-start = ((), (), s32[]{:S(2)}) async-start(), calls=%async_computation.2 | async-start | bytes 18874368 | tf_op jit(solution)/shard_map/all_gather | solution.py:13
Sparse Core Ops, SparseCore 0:
  8.9 60.9 all-gather.2
  72.0 227.2 all-gather.4
where the time goes:
time: 345 us
  waiting for transfers between devices  293 us (85%)
  matrix products  30.4 us (9%)
  between operations  13.4 us (4%)
  blocking collectives  6.49 us (2%)
    all_gather x1, waiting for transfers between devices, shards(): lax.all_gather(wave, 'row', axis=0, tiled=True)  229 us
    all_gather x1, waiting for transfers between devices, shards(): env_full = lax.all_gather(env, 'col', axis=1, tiled=True)  61.9 us
    dot_general x1, matrix products, shards(): jnp.dot(env_full, lax.all_gather(wave, 'row', axis=0, tiled=True), precis...  30.2 us
  transfers between devices with their start and end apart: 2, of which 2 were waited for; matrix products, arithmetic and copies ran while one was open for 0% of the time, Pallas kernels for 0%

commit v1 on v0

--- a/solution.py
+++ b/solution.py
@@ -6,7 +6,7 @@
 
 def shards(env, wave, mpo):
     spins = mpo.shape[0]
-    env_full = lax.all_gather(env, "col", axis=1, tiled=True)
+    env_full = jnp.concatenate(lax.all_gather(env, "col"), axis=1)
     right_local = wave.shape[1] // spins
     partial_out = jnp.dot(
         env_full,

time: 345 us -> 333 us (0.965)
  waiting for transfers between devices: 293 us -> 266 us
  local copies, waits for them, and re-layouts: 1.44 us -> 28.4 us
  matrix products: 30.4 us -> 17.3 us
    all_gather x1, waiting for transfers between devices: 229 us -> 205 us  [shards(): lax.all_gather(wave, 'row', axis=0, tiled=True)]
    dot_general x1, matrix products: 30.2 us -> 17 us  [shards(): jnp.dot(env_full, lax.all_gather(wave, 'row', axis=0, tiled=True), precis...]
    all_gather x0 -> x1, local copies, waits for them, and re-layouts: none -> 12.9 us  [shards(): env_full = jnp.concatenate(lax.all_gather(env, 'col'), axis=1)]
    reshape x0 -> x1, local copies, waits for them, and re-layouts: none -> 11.1 us  [shards(): env_full = jnp.concatenate(lax.all_gather(env, 'col'), axis=1)]
  transfers between devices with their start and end apart: 2 -> 2, of which waited for: 2 -> 2; matrix products, arithmetic and copies ran while one was open for 0% -> 8% of each run, Pallas kernels for 0% -> 0%
where the time goes in v1:
time: 333 us; the launch traced here: 332 us
  waiting for transfers between devices  266 us (80%)
  local copies, waits for them, and re-layouts  28.4 us (9%)
  matrix products  17.3 us (5%)
  between operations  13.4 us (4%)
  blocking collectives  6.48 us (2%)
    all_gather x1, waiting for transfers between devices, shards(): lax.all_gather(wave, 'row', axis=0, tiled=True)  205 us
    all_gather x1, waiting for transfers between devices, shards(): env_full = jnp.concatenate(lax.all_gather(env, 'col'), axis=1)  59.6 us
    dot_general x1, matrix products, shards(): jnp.dot(env_full, lax.all_gather(wave, 'row', axis=0, tiled=True), precis...  17 us
    all_gather x1, local copies, waits for them, and re-layouts, shards(): env_full = jnp.concatenate(lax.all_gather(env, 'col'), axis=1)  12.9 us
    reshape x1, local copies, waits for them, and re-layouts, shards(): env_full = jnp.concatenate(lax.all_gather(env, 'col'), axis=1)  11.1 us
  transfers between devices with their start and end apart: 2, of which 2 were waited for; matrix products, arithmetic and copies ran while one was open for 8% of the time, Pallas kernels for 0%

profile of v1, /device:TPU:0, one launch (start us, length us, event | category | flops | bytes accessed | tf_op | source)
XLA Modules:
  0.0 332.2 jit_solution(18391022044281780472)
XLA Ops:
  6.5 0.0 copy-start
  6.5 0.0 all-gather.6.cloned.1.call-start
  6.5 0.7 all-gather.6.cloned.1.call-update
  7.3 0.0 all-gather.4.cloned.1.call-start
  7.3 2.9 copy.12
  10.2 0.0 all-gather.4.cloned.1.call-update
  10.3 59.6 %all-gather.6.cloned.1.call-done = f32[256,8192]{1,0:T(8,128)} async-done(((f32[64,8192]{1,0:T(8,128)}), f32[256,8192]{1,0:T(8,128)}) %all-gather.6.cloned.1.call-update) | async-done | bytes 8388624 | tf_op jit(solution)/shard_map/all_gather | solution.py:9
  69.9 12.9 %copy.21 = f32[4,64,8192]{2,0,1:T(4,128)} copy(f32[4,64,8192]{2,1,0:T(8,128)} %bitcast.25) | data formatting | bytes 16777216 | tf_op jit(solution)/shard_map/all_gather | solution.py:9
  82.8 11.1 %reshape.16 = f32[64,32768,1]{1,0,2:T(8,128)} reshape(f32[64,4,8192]{2,1,0:T(4,128)} %bitcast.23) | data formatting | bytes 16777216 | tf_op jit(solution)/shard_map/reshape | solution.py:9
  93.9 205.5 %all-gather.4.cloned.1.call-done = f32[32768,128]{0,1:T(8,128)} async-done(((f32[4096,128]{0,1:T(8,128)}), f32[32768,128]{0,1:T(8,128)}) %all-gather.4.cloned.1.call-update) | async-done | bytes 16777232 | tf_op jit(solution)/shard_map/all_gather | solution.py:13
  299.4 17.0 %fusion.1 = f32[64,8,16]{0,2,1:T(8,128)S(1)} fusion(f32[64,32768,1]{1,0,2:T(8,128)} %reshape.16, f32[8,16,32768]{2,1,0:T(8,128)} %bitcast.24), kind=kOutput, calls=%fused_computation.4 | convolution fusion | flops 3221225472 | bytes 25198592 | tf_op jit(solution)/shard_map/dot_general | solution.py:11
  316.4 0.0 copy-done
  316.4 0.3 convolution_bitcast_fusion
  316.7 0.1 reshape.19
  316.8 6.5 %all_to_all.15 = f32[4,1,2048]{2,1,0:T(1,128)S(1)} all-to-all(f32[4,1,2048]{2,1,0:T(1,128)S(1)} %reshape.19), channel_id=1, replica_groups=mesh['row'=8,'col'=4] {'col'}, dimensions={0} | all-to-all | bytes 65536 | tf_op jit(solution)/shard_map/all_to_all | solution.py:19
  323.3 0.5 broadcast
  323.8 0.7 reduce
  324.6 0.1 reshape.20
  324.7 0.7 copy.16
  (2 shorter events, 0.0 us)
Async XLA Ops:
  6.5 309.9 %copy-start = (f32[16,16]{1,0:T(8,128)S(1)}, f32[16,16]{1,0:T(8,128)}, u32[]{:S(2)}) copy-start(f32[16,16]{1,0:T(8,128)} %param.5) | copy-start | bytes 3076
  6.5 63.4 %all-gather.6.cloned.1.call-start = ((), (), s32[]{:S(2)}) async-start(), calls=%async_computation.2 | async-start | bytes 10485760 | tf_op jit(solution)/shard_map/all_gather | solution.py:9
  7.3 292.1 %all-gather.4.cloned.1.call-start = ((), (), s32[]{:S(2)}) async-start(), calls=%async_computation.1 | async-start | bytes 18874368 | tf_op jit(solution)/shard_map/all_gather | solution.py:13
Sparse Core Ops, SparseCore 0:
  8.9 60.9 all-gather.5
  72.1 227.2 all-gather.3

commit v2 on v0

--- a/solution.py
+++ b/solution.py
@@ -10,7 +10,9 @@
     right_local = wave.shape[1] // spins
     partial_out = jnp.dot(
         env_full,
-        lax.all_gather(wave, "row", axis=0, tiled=True),
+        jnp.concatenate(
+            lax.all_to_all(jnp.stack([wave] * lax.axis_size("row")), "row", 0, 0), axis=0
+        ),
         precision=lax.Precision.HIGHEST,
         preferred_element_type=jnp.float32,
     )

time: 345 us -> 431 us (1.25)
  waiting for transfers between devices: 293 us -> 363 us
  local copies, waits for them, and re-layouts: 1.44 us -> 22.9 us
  matrix products: 30.4 us -> 17.3 us
  starting transfers between devices: 0.04 us -> 7.35 us
    all_to_all x0 -> x1, waiting for transfers between devices: none -> 362 us  [shards(): lax.all_to_all(jnp.stack([wave] * lax.axis_size('row')), 'row', 0, 0)]
    all_gather x1 -> x0, waiting for transfers between devices: 229 us -> none  [shards(): lax.all_gather(wave, 'row', axis=0, tiled=True)]
    all_gather x1, waiting for transfers between devices: 61.9 us -> 0.01 us  [shards(): env_full = lax.all_gather(env, 'col', axis=1, tiled=True)]
    dot_general x1, matrix products: 30.2 us -> 17 us  [shards(): jnp.dot(env_full, jnp.concatenate(lax.all_to_all(jnp.stack([wave] * lax.a...]
    reshape x0 -> x1, local copies, waits for them, and re-layouts: none -> 11.6 us  [shards(): jnp.concatenate(lax.all_to_all(jnp.stack([wave] * lax.axis_size('row')),...]
    another operation x0 -> x1, local copies, waits for them, and re-layouts: none -> 8.01 us  [shards(): jnp.stack([wave] * lax.axis_size('row'))]
    all_to_all x0 -> x1, starting transfers between devices: none -> 7.31 us  [shards(): lax.all_to_all(jnp.stack([wave] * lax.axis_size('row')), 'row', 0, 0)]
  transfers between devices with their start and end apart: 2 -> 2, of which waited for: 2 -> 1; matrix products, arithmetic and copies ran while one was open for 0% -> 3% of each run, Pallas kernels for 0% -> 0%
where the time goes in v2:
time: 431 us
  waiting for transfers between devices  363 us (84%)
  local copies, waits for them, and re-layouts  22.9 us (5%)
  matrix products  17.3 us (4%)
  between operations  13.4 us (3%)
  starting transfers between devices  7.35 us (2%)
  blocking collectives  6.53 us (2%)
    all_to_all x1, waiting for transfers between devices, shards(): lax.all_to_all(jnp.stack([wave] * lax.axis_size('row')), 'row', 0, 0)  362 us
    dot_general x1, matrix products, shards(): jnp.dot(env_full, jnp.concatenate(lax.all_to_all(jnp.stack([wave] * lax.a...  17 us
    reshape x1, local copies, waits for them, and re-layouts, shards(): jnp.concatenate(lax.all_to_all(jnp.stack([wave] * lax.axis_size('row')),...  11.6 us
  transfers between devices with their start and end apart: 2, of which 1 were waited for; matrix products, arithmetic and copies ran while one was open for 3% of the time, Pallas kernels for 0%

profile of v2, /device:TPU:0, one launch (start us, length us, event | category | flops | bytes accessed | tf_op | source)
XLA Modules:
  0.0 431.2 jit_solution(17038310583289702271)
XLA Ops:
  6.5 0.0 copy-start
  6.5 1.9 copy.10
  8.5 8.0 %stack.2 = f32[8,4096,128]{1,2,0:T(8,128)} broadcast(f32[4096,128]{0,1:T(8,128)S(1)} %copy.10), dimensions={1,2} | broadcast | bytes 18874368 | tf_op jit(solution)/shard_map/stack | solution.py:14
  16.5 7.3 %all-to-all-start = ((f32[8,4096,128]{1,2,0:T(8,128)}), f32[8,4096,128]{1,2,0:T(8,128)}, u32[]{:S(2)}, u32[]{:S(2)}) async-start(f32[8,4096,128]{1,2,0:T(8,128)} %stack.2), calls=%async_computation | async-start | bytes 33554432 | tf_op jit(solution)/shard_map/all_to_all | solution.py:14
  23.8 0.0 all-gather.2.cloned.1.call-start
  23.8 0.7 all-gather.2.cloned.1.call-update
  24.5 362.3 %all-to-all-done = f32[8,4096,128]{1,2,0:T(8,128)} async-done(((f32[8,4096,128]{1,2,0:T(8,128)}), f32[8,4096,128]{1,2,0:T(8,128)}, u32[]{:S(2)}, u32[]{:S(2)}) %all-to-all-start) | async-done | bytes 16777248 | tf_op jit(solution)/shard_map/all_to_all | solution.py:14
  386.8 11.6 %copy.18 = f32[8,16,8,4096]{3,2,0,1:T(8,128)} copy(f32[8,16,8,4096]{3,2,1,0:T(8,128)} %bitcast.10) | data formatting | bytes 33554432 | tf_op jit(solution)/shard_map/reshape | solution.py:13
  398.4 0.0 all-gather.2.cloned.1.call-done
  398.4 17.0 %fusion = f32[64,8,16]{0,2,1:T(8,128)S(1)} fusion(f32[8,16,32768]{2,1,0:T(8,128)} %bitcast.24, f32[64,32768]{1,0:T(8,128)} %all-gather.2.cloned.1.call-done), kind=kOutput, calls=%fused_computation | convolution fusion | flops 3221225472 | bytes 25198592 | tf_op jit(solution)/shard_map/dot_general | solution.py:11
  415.4 0.0 copy-done
  415.4 0.3 convolution_bitcast_fusion
  415.7 0.1 reshape.15
  415.8 6.5 %all_to_all.20 = f32[4,1,2048]{2,1,0:T(1,128)S(1)} all-to-all(f32[4,1,2048]{2,1,0:T(1,128)S(1)} %reshape.15), channel_id=1, replica_groups=mesh['row'=8,'col'=4] {'col'}, dimensions={0} | all-to-all | bytes 65536 | tf_op jit(solution)/shard_map/all_to_all | solution.py:21
  422.3 0.5 broadcast.2
  422.8 0.7 reduce
  423.6 0.1 reshape.16
  423.7 0.7 copy.15
  (2 shorter events, 0.0 us)
Async XLA Ops:
  6.5 408.9 %copy-start = (f32[16,16]{1,0:T(8,128)S(1)}, f32[16,16]{1,0:T(8,128)}, u32[]{:S(2)}) copy-start(f32[16,16]{1,0:T(8,128)} %param.5) | copy-start | bytes 3076
  16.5 370.3 %all-to-all-start = ((f32[8,4096,128]{1,2,0:T(8,128)}), f32[8,4096,128]{1,2,0:T(8,128)}, u32[]{:S(2)}, u32[]{:S(2)}) async-start(f32[8,4096,128]{1,2,0:T(8,128)} %stack.2), calls=%async_computation | async-start | bytes 33554432 | tf_op jit(solution)/shard_map/all_to_all | solution.py:14
  23.8 374.6 %all-gather.2.cloned.1.call-start = ((), (), s32[]{:S(2)}) async-start(), calls=%async_computation.2 | async-start | bytes 10485760 | tf_op jit(solution)/shard_map/all_gather | solution.py:9
Sparse Core Ops, SparseCore 0:
  26.2 59.6 all-gather.1
